TPU v7x, 512 devices: a whole 4x4x16 slice. The times are simulated.
512 devices in a mesh: lon: 16 (over z), lat: 8 (over x_lo, y), ch: 4 (over x_hi, core).
Axes of the slice: x: 4 (x_hi: 2, x_lo: 2; x = x_hi * 2 + x_lo), y: 4, z: 16, core: 2. Of those that a mesh axis runs over, the one named last changes fastest.
Arguments:
- ocean_state: bfloat16 [300, 256, 2048], P('ch', 'lat', 'lon'), may hold values from -6 to 6
- land_mask: int32 [256, 2048], P('lat', 'lon'), may hold values 0 or 1
- out_grad: bfloat16 [300, 256, 2048], P('ch', 'lat', 'lon'), may hold values from -6 to 6
- swath_offset: int32 [8, 16, 512], P('lat', 'lon'), may hold values from 0 to 4095
- swath_value: float32 [8, 16, 512], P('lat', 'lon'), may hold values from -8 to 8
- depth_kernel: float32 [3, 3, 300], P(None, None, 'ch'), may hold values from -2.5 to 2.5
- expand_weight: bfloat16 [300, 600], P(None, 'ch'), may hold values from -0.375 to 0.375
- expand_bias: float32 [600], P('ch'), may hold values from -3 to 3
- project_weight: bfloat16 [600, 300], P('ch'), may hold values from -0.25 to 0.25
Outputs:
- state_grad: bfloat16 [300, 256, 2048], P('ch', 'lat', 'lon')
- expand_grad: float32 [300, 600], P(None, 'ch')
- project_grad: float32 [600, 300], P('ch')
- bias_grad: float32 [600], P('ch')
- kernel_grad: float32 [3, 3, 300], P(None, None, 'ch')
Inputs may be any that keep to these rules, and one draw needn't show every extreme that they name: `swath_offset`: position of a swath point in row-major order over the 32 x 128 cells of its device's block.
All inputs are finite; a program needn't handle non-finite values. No bound on the sum of `land_mask` on one device may be relied on, other than what follows from the above.
Results may differ from a plain program's by a relative error of at most 0.014.
Values may be sent and summed in bfloat16 or wider, within the bound.
A program may use at most 64 MiB of HBM per device.

v0:
```python
import math
import jax
import jax.numpy as jnp
from jax import lax
from jax.sharding import PartitionSpec as P

DILATION_STEP = 2


def with_halo(block, sides, width):
    for axis, dim in sides:
        count = lax.axis_size(axis)
        forward = [(i, i + 1) for i in range(count - 1)]
        forward.append((count - 1, 0))
        backward = [(target, source) for source, target in forward]
        low = lax.ppermute(
            lax.slice_in_dim(block, block.shape[dim] - width, None, axis=dim), axis, forward
        )
        high = lax.ppermute(lax.slice_in_dim(block, 0, width, axis=dim), axis, backward)
        block = jnp.concatenate([low, block, high], axis=dim)
    return block


def extend(ocean_field):
    count_of_rows = ocean_field.shape[1]
    column_count = ocean_field.shape[2]
    halo_padded = with_halo(ocean_field, (("lon", 2), ("lat", 1)), DILATION_STEP)
    uppermost_rows = ocean_field[:, count_of_rows - DILATION_STEP :, :]
    gathered = lax.all_gather(uppermost_rows, "lon", axis=2, tiled=True)
    seam_mirrored = gathered[:, ::-1, ::-1]
    seam_mirrored = jnp.concatenate(
        [seam_mirrored[:, :, -DILATION_STEP:], seam_mirrored, seam_mirrored[:, :, :DILATION_STEP]],
        axis=2,
    )
    northern_border = lax.dynamic_slice_in_dim(
        seam_mirrored, lax.axis_index("lon") * column_count, column_count + 2 * DILATION_STEP, 2
    )
    latitude_index = lax.axis_index("lat")
    southern_boundary = halo_padded[:, :DILATION_STEP, :]
    southern_border = jnp.where(
        latitude_index == 0, jnp.zeros_like(southern_boundary), southern_boundary
    )
    northern_border = jnp.where(
        latitude_index == lax.axis_size("lat") - 1,
        northern_border,
        halo_padded[:, count_of_rows + DILATION_STEP :, :],
    )
    return jnp.concatenate(
        [
            southern_border,
            halo_padded[:, DILATION_STEP : count_of_rows + DILATION_STEP, :],
            northern_border,
        ],
        axis=1,
    )


def on_device(
    ocean_state,
    land_mask,
    out_grad,
    swath_offset,
    swath_value,
    depth_kernel,
    expand_weight,
    expand_bias,
    project_weight,
):
    channels_per_shard = ocean_state.shape[0]
    count_of_rows = ocean_state.shape[1]
    column_count = ocean_state.shape[2]
    cells = count_of_rows * column_count
    scale = 1.0 / math.sqrt(
        count_of_rows * lax.axis_size("lat") * column_count * lax.axis_size("lon")
    )
    mask_float = land_mask.astype(jnp.float32)[None]
    masked = ocean_state * land_mask.astype(jnp.bfloat16)[None]
    state_pad = extend(masked)
    forward = jnp.zeros((channels_per_shard, count_of_rows, column_count), jnp.float32)
    for row_offset in range(3):
        for column_offset in range(3):
            kernel_window = state_pad[
                :,
                DILATION_STEP * row_offset : DILATION_STEP * row_offset + count_of_rows,
                DILATION_STEP * column_offset : DILATION_STEP * column_offset + column_count,
            ]
            forward = forward + depth_kernel[row_offset, column_offset][
                :, None, None
            ] * kernel_window.astype(jnp.float32)
    conv_out = forward.astype(jnp.bfloat16)
    swath = (
        jnp.zeros((cells,), jnp.float32).at[swath_offset.reshape(-1)].add(swath_value.reshape(-1))
    )
    first_group = jnp.where(lax.axis_index("ch") == 0, 1.0, 0.0).astype(jnp.float32)
    cotan = (
        out_grad.astype(jnp.float32)
        .at[0]
        .add(first_group * swath.reshape(count_of_rows, column_count))
    )
    cotan = (cotan * mask_float).astype(jnp.bfloat16)
    conv_all, cotan_all = (
        lax.all_gather(conv_out, "ch", axis=0, tiled=True),
        lax.all_gather(cotan, "ch", axis=0, tiled=True),
    )
    conv_flat = conv_all.reshape(conv_all.shape[0], cells)
    cotan_flat = cotan_all.reshape(cotan_all.shape[0], cells)
    hidden = (
        jnp.dot(expand_weight.T, conv_flat, preferred_element_type=jnp.float32)
        + expand_bias[:, None]
    )
    activ, gelu_back = jax.vjp(jax.nn.gelu, hidden)
    act_grad = jnp.dot(project_weight, cotan_flat, preferred_element_type=jnp.float32)
    pre_grad = gelu_back(act_grad)[0].astype(jnp.bfloat16)
    project_part = (
        jnp.dot(activ.astype(jnp.bfloat16), cotan_flat.T, preferred_element_type=jnp.float32)
        * scale
    )
    expand_part = jnp.dot(conv_flat, pre_grad.T, preferred_element_type=jnp.float32) * scale
    bias_part = jnp.sum(pre_grad.astype(jnp.float32), axis=1) * scale
    summed = lax.psum_scatter(
        jnp.dot(expand_weight, pre_grad, preferred_element_type=jnp.float32).astype(jnp.bfloat16),
        "ch",
        scatter_dimension=0,
        tiled=True,
    )
    conv_grad = summed.reshape(channels_per_shard, count_of_rows, column_count)
    grad_pad = extend(conv_grad)
    grad_float = conv_grad.astype(jnp.float32)
    kernel_rows = []
    swapped_axes = jnp.zeros((channels_per_shard, count_of_rows, column_count), jnp.float32)
    for row_offset in range(3):
        kernel_cols = []
        for column_offset in range(3):
            kernel_window = state_pad[
                :,
                DILATION_STEP * row_offset : DILATION_STEP * row_offset + count_of_rows,
                DILATION_STEP * column_offset : DILATION_STEP * column_offset + column_count,
            ]
            kernel_cols.append(jnp.sum(grad_float * kernel_window.astype(jnp.float32), axis=(1, 2)))
            reverse_row = DILATION_STEP * (2 - row_offset)
            reverse_column = DILATION_STEP * (2 - column_offset)
            back_window = grad_pad[
                :,
                reverse_row : reverse_row + count_of_rows,
                reverse_column : reverse_column + column_count,
            ]
            swapped_axes = swapped_axes + depth_kernel[row_offset, column_offset][
                :, None, None
            ] * back_window.astype(jnp.float32)
        kernel_rows.append(jnp.stack(kernel_cols, axis=0))
    kernel_part = jnp.stack(kernel_rows, axis=0) * scale
    fold_adjustment = jnp.zeros((channels_per_shard, DILATION_STEP, column_count), jnp.float32)
    for column_offset in range(3):
        reverse_column = DILATION_STEP * (2 - column_offset)
        rim_window = grad_pad[
            :,
            count_of_rows + DILATION_STEP : count_of_rows + 2 * DILATION_STEP,
            reverse_column : reverse_column + column_count,
        ]
        weight_change = depth_kernel[2, 2 - column_offset] - depth_kernel[0, column_offset]
        fold_adjustment = fold_adjustment + weight_change[:, None, None] * rim_window.astype(
            jnp.float32
        )
    at_top = lax.axis_index("lat") == lax.axis_size("lat") - 1
    swapped_axes = swapped_axes.at[:, count_of_rows - DILATION_STEP :, :].add(
        jnp.where(at_top, fold_adjustment, jnp.zeros_like(fold_adjustment))
    )
    state_grad = (mask_float * (cotan.astype(jnp.float32) + swapped_axes)).astype(jnp.bfloat16)
    expand_grad, project_grad, bias_grad, kernel_grad = lax.psum(
        (expand_part, project_part, bias_part, kernel_part), ("lon", "lat")
    )
    return (state_grad, expand_grad, project_grad, bias_grad, kernel_grad)


def solution(mesh):
    return jax.shard_map(
        on_device,
        mesh=mesh,
        in_specs=(
            P("ch", "lat", "lon"),
            P("lat", "lon"),
            P("ch", "lat", "lon"),
            P("lat", "lon", None),
            P("lat", "lon", None),
            P(None, None, "ch"),
            P(None, "ch"),
            P("ch"),
            P("ch", None),
        ),
        out_specs=(
            P("ch", "lat", "lon"),
            P(None, "ch"),
            P("ch", None),
            P("ch"),
            P(None, None, "ch"),
        ),
        check_vma=False,
    )
```

profile of v0, /device:TPU:4, one launch (start us, length us, event | category | flops | bytes accessed | tf_op | source)
XLA Modules:
  0.0 1292.7 jit_solution(13573045520863102719)
XLA Ops:
  10.0 3.4 scatter_custom_fusion
  16.0 11.4 collective-permute-start.1
  30.1 32.5 %all_gather.13 = bf16[75,2,2048]{2,1,0:T(2,128)(2,1)S(1)} all-gather(bf16[75,2,128]{2,1,0:T(2,128)(2,1)S(1)} %slice.277), channel_id=1, replica_groups=mesh['lon'=16,'lat'=8,'ch'=4] {'lon'}, dimensions={2}, use_global_device_ids=true | all-gather | bytes 652800 | tf_op jit(solution)/shard_map/all_gather | solution.py:29
  65.4 3.5 collective-permute-start.2
  69.5 5.5 rev.6
  75.7 4.0 concatenate.54
  79.7 4.5 collective-permute-start.3
  91.3 4.1 fusion.19
  101.5 23.7 %all-gather.5.cloned.1.call-done = bf16[300,32,128]{2,1,0:T(8,128)(2,1)} async-done(((bf16[75,32,128]{2,1,0:T(8,128)(2,1)}), bf16[300,32,128]{2,1,0:T(8,128)(2,1)}) %all-gather.5.cloned.1.call-update) | async-done | bytes 2457616 | tf_op jit(solution)/shard_map/all_gather | solution.py:102
  138.9 31.6 %fusion = bf16[80,4096]{1,0:T(8,128)(2,1)} fusion(bf16[300,4096]{1,0:T(8,128)(2,1)S(1)} %fusion.2), kind=kCustom, calls=%all-reduce-scatter | all-reduce-scatter fusion | flops 1310721 | bytes 3115008
  173.9 5.3 collective-permute-done.8
  179.2 6.0 concatenate.62
  186.9 4.9 fusion.28
  192.2 34.5 %all_gather.15 = bf16[75,2,2048]{2,1,0:T(2,128)(2,1)S(1)} all-gather(bf16[75,2,128]{2,1,0:T(2,128)(2,1)S(1)} %slice.285), channel_id=1, replica_groups=mesh['lon'=16,'lat'=8,'ch'=4] {'lon'}, dimensions={2}, use_global_device_ids=true | all-gather | bytes 652800 | tf_op jit(solution)/shard_map/all_gather | solution.py:29
  228.3 3.0 collective-permute-start.5
  231.3 2.8 collective-permute-start.4
  234.4 3.8 collective-permute-done.4
  240.7 3.2 collective-permute-start.7
  244.0 5.5 rev.7
  250.1 4.0 concatenate.57
  254.2 311.0 %all-reduce.2 = (f32[150]{0:T(256)}, f32[3,3,75]{2,1,0:T(4,128)}) all-reduce(f32[150]{0:T(256)S(1)} %copy-done.33, f32[3,3,75]{2,1,0:T(4,128)S(1)} %maximum_multiply_fusion), channel_id=1, replica_groups=mesh['lon'=16,'lat'=8,'ch'=4] {'lon','lat'}, use_global_device_ids=true, to_apply=%region_5.6 | all-reduce | flops 825 | bytes 6600 | tf_op jit(solution)/shard_map/psum | solution.py:169
  567.2 4.3 collective-permute-done.6
  575.2 3.4 fusion.24
  580.2 702.8 %all-reduce.6.cloned.1.call-done = (f32[300,150]{0,1:T(8,128)}, f32[150,300]{1,0:T(8,128)}) async-done(((f32[300,150]{0,1:T(8,128)}, f32[150,300]{1,0:T(8,128)}), (f32[300,150]{0,1:T(8,128)}, f32[150,300]{1,0:T(8,128)})) %all-reduce.6.cloned.1.call-update) | async-done | bytes 360016 | tf_op jit(solution)/shard_map/psum | solution.py:169
  (166 shorter events, 58.8 us)
Async XLA Ops:
  7.2 121.4 %copy-start = (bf16[300,150]{0,1:T(8,128)(2,1)S(1)}, bf16[300,150]{0,1:T(8,128)(2,1)}, u32[]{:S(2)}) copy-start(bf16[300,150]{0,1:T(8,128)(2,1)} %param.19) | copy-start | bytes 270004
  7.2 91.0 %all-gather.3.cloned.1.call-start = ((), (), s32[]{:S(2)}) async-start(), calls=%async_computation | async-start | bytes 3072000 | tf_op jit(solution)/shard_map/all_gather | solution.py:103
  14.4 110.8 %all-gather.5.cloned.1.call-start = ((), (), s32[]{:S(2)}) async-start(), calls=%async_computation.1 | async-start | bytes 3072000 | tf_op jit(solution)/shard_map/all_gather | solution.py:102
  16.0 47.9 %collective-permute-start.1 = (bf16[75,32,2]{0,1,2:T(8,128)(2,1)S(1)}, bf16[75,32,2]{0,1,2:T(8,128)(2,1)S(1)}, u32[]{:S(2)}, u32[]{:S(2)}) collective-permute-start(bf16[75,32,2]{0,1,2:T(8,128)(2,1)S(1)} %copy.31), channel_id=1, source_target_pairs={{32,0},{64,32},{96,64},{128,96},{160,128},{192,160},{224,192},{256... | collective-permute-start | bytes 28808 | tf_op jit(solution)/shard_map/ppermute | solution.py:19
  28.2 34.6 %collective-permute-start = (bf16[75,32,2]{0,1,2:T(8,128)(2,1)S(1)}, bf16[75,32,2]{0,1,2:T(8,128)(2,1)S(1)}, u32[]{:S(2)}, u32[]{:S(2)}) collective-permute-start(bf16[75,32,2]{0,1,2:T(8,128)(2,1)S(1)} %copy.30), channel_id=1, source_target_pairs={{0,32},{32,64},{64,96},{96,128},{128,160},{160,192},{192,224},{224... | collective-permute-start | bytes 28808 | tf_op jit(solution)/shard_map/ppermute | solution.py:16
  63.8 25.8 %copy-start.5 = (bf16[75,32,2]{2,1,0:T(8,128)(2,1)}, bf16[75,32,2]{2,1,0:T(8,128)(2,1)S(1)}, u32[]{:S(2)}) copy-start(bf16[75,32,2]{2,1,0:T(8,128)(2,1)S(1)} %copy.32) | copy-start | bytes 28804
  64.9 24.7 %copy-start.7 = (bf16[75,32,2]{2,1,0:T(8,128)(2,1)}, bf16[75,32,2]{2,1,0:T(8,128)(2,1)S(1)}, u32[]{:S(2)}) copy-start(bf16[75,32,2]{2,1,0:T(8,128)(2,1)S(1)} %copy.33) | copy-start | bytes 28804
  65.4 18.8 %collective-permute-start.2 = (bf16[75,2,132]{2,1,0:T(2,128)(2,1)S(1)}, bf16[75,2,132]{2,1,0:T(2,128)(2,1)}, u32[]{:S(2)}, u32[]{:S(2)}) collective-permute-start(bf16[75,2,132]{2,1,0:T(2,128)(2,1)S(1)} %get-tuple-element.51), channel_id=1, source_target_pairs={{0,4},{4,8},{8,12},{12,16},{16,20},{20,24},{24,28},{28,0},{1,5},{5... | collective-permute-start | bytes 118808 | tf_op jit(solution)/shard_map/ppermute | solution.py:16
  79.7 6.5 collective-permute-start.3
  95.4 1187.5 %all-reduce.6.cloned.1.call-start = ((), (), s32[]{:S(2)}) async-start(), calls=%async_computation.2 | async-start | bytes 933888 | tf_op jit(solution)/shard_map/psum | solution.py:169
  171.4 7.8 collective-permute-start.8
  192.1 42.1 %copy-start.34 = (f32[75]{0:T(128)S(1)}, f32[75]{0:T(128)}, u32[]{:S(2)}) copy-start(f32[75]{0:T(128)} %get-tuple-element.35) | copy-start | bytes 904
  192.1 42.1 %copy-start.35 = (f32[75]{0:T(128)S(1)}, f32[75]{0:T(128)}, u32[]{:S(2)}) copy-start(f32[75]{0:T(128)} %get-tuple-element.36) | copy-start | bytes 904
  192.1 42.1 %copy-start.36 = (f32[75]{0:T(128)S(1)}, f32[75]{0:T(128)}, u32[]{:S(2)}) copy-start(f32[75]{0:T(128)} %get-tuple-element.37) | copy-start | bytes 904
  192.1 42.1 %copy-start.37 = (f32[75]{0:T(128)S(1)}, f32[75]{0:T(128)}, u32[]{:S(2)}) copy-start(f32[75]{0:T(128)} %get-tuple-element.56) | copy-start | bytes 904
  192.1 42.1 %copy-start.38 = (f32[75]{0:T(128)S(1)}, f32[75]{0:T(128)}, u32[]{:S(2)}) copy-start(f32[75]{0:T(128)} %get-tuple-element.57) | copy-start | bytes 904
  192.1 42.1 %copy-start.39 = (f32[75]{0:T(128)S(1)}, f32[75]{0:T(128)}, u32[]{:S(2)}) copy-start(f32[75]{0:T(128)} %get-tuple-element.58) | copy-start | bytes 904
  192.1 42.1 %copy-start.43 = (f32[75]{0:T(128)S(1)}, f32[75]{0:T(128)}, u32[]{:S(2)}) copy-start(f32[75]{0:T(128)} %get-tuple-element.53) | copy-start | bytes 904
  192.2 42.1 %copy-start.44 = (f32[75]{0:T(128)S(1)}, f32[75]{0:T(128)}, u32[]{:S(2)}) copy-start(f32[75]{0:T(128)} %get-tuple-element.54) | copy-start | bytes 904
  192.2 42.1 %copy-start.45 = (f32[75]{0:T(128)S(1)}, f32[75]{0:T(128)}, u32[]{:S(2)}) copy-start(f32[75]{0:T(128)} %get-tuple-element.55) | copy-start | bytes 904
  228.3 10.9 collective-permute-start.5
  231.3 6.8 collective-permute-start.4
  240.7 326.4 %collective-permute-start.7 = (bf16[75,2,132]{2,1,0:T(2,128)(2,1)S(1)}, bf16[75,2,132]{2,1,0:T(2,128)(2,1)}, u32[]{:S(2)}, u32[]{:S(2)}) collective-permute-start(bf16[75,2,132]{2,1,0:T(2,128)(2,1)S(1)} %get-tuple-element.48), channel_id=1, source_target_pairs={{0,4},{4,8},{8,12},{12,16},{16,20},{20,24},{24,28},{28,0},{1,5},{5... | collective-permute-start | bytes 118808 | tf_op jit(solution)/shard_map/ppermute | solution.py:16
  565.2 6.3 collective-permute-start.6
  (35 other events, 219.6 us)
Sparse Core Ops, SparseCore 0:
  14.5 38.0 all-gather.2
  95.5 29.6 all-gather.4
  173.5 1109.3 all-reduce.5
where the time goes:
time: 1290 us
  waiting for transfers between devices  742 us (58%)
  blocking collectives  410 us (32%)
  local copies, waits for them, and re-layouts  52.1 us (4%)
  starting transfers between devices  34.4 us (3%)
  other arithmetic  30.2 us (2%)
  between operations  15.4 us (1%)
    psum x1, waiting for transfers between devices, on_device(): lax.psum((expand_part, project_part, bias_part, kernel_part), ('lon', 'la...  703 us
    psum x1, blocking collectives, on_device(): lax.psum((expand_part, project_part, bias_part, kernel_part), ('lon', 'la...  311 us
    all_gather x2, blocking collectives, extend(): gathered = lax.all_gather(uppermost_rows, 'lon', axis=2, tiled=True)  67 us
    unnamed x1, blocking collectives  31.6 us
  transfers between devices with their start and end apart: 12, of which 6 were waited for; matrix products, arithmetic and copies ran while one was open for 5% of the time, Pallas kernels for 0%

commit v1 on v0

--- a/solution.py
+++ b/solution.py
@@ -26,7 +26,10 @@
     column_count = ocean_field.shape[2]
     halo_padded = with_halo(ocean_field, (("lon", 2), ("lat", 1)), DILATION_STEP)
     uppermost_rows = ocean_field[:, count_of_rows - DILATION_STEP :, :]
-    gathered = lax.all_gather(uppermost_rows, "lon", axis=2, tiled=True)
+    n_dev = lax.axis_size("lon")
+    tiles = jnp.stack([uppermost_rows for _ in range(n_dev)])
+    tiles = lax.all_to_all(tiles, "lon", split_axis=0, concat_axis=0)
+    gathered = jnp.concatenate(tiles, axis=2)
     seam_mirrored = gathered[:, ::-1, ::-1]
     seam_mirrored = jnp.concatenate(
         [seam_mirrored[:, :, -DILATION_STEP:], seam_mirrored, seam_mirrored[:, :, :DILATION_STEP]],

time: 1290 us -> 1320 us (1.023)
  blocking collectives: 410 us -> 346 us
  waiting for transfers between devices: 742 us -> 790 us
  starting transfers between devices: 34.4 us -> 57.6 us
    all_gather x2 -> x0, blocking collectives: 67 us -> none  [extend(): gathered = lax.all_gather(uppermost_rows, 'lon', axis=2, tiled=True)]
    psum x1, waiting for transfers between devices: 703 us -> 745 us  [on_device(): lax.psum((expand_part, project_part, bias_part, kernel_part), ('lon', 'la...]
    all_to_all x0 -> x2, starting transfers between devices: none -> 27.5 us  [extend(): tiles = lax.all_to_all(tiles, 'lon', split_axis=0, concat_axis=0)]
  transfers between devices with their start and end apart: 12 -> 14, of which waited for: 6 -> 5; matrix products, arithmetic and copies ran while one was open for 5% -> 6% of each run, Pallas kernels for 0% -> 0%
where the time goes in v1:
time: 1320 us
  waiting for transfers between devices  790 us (60%)
  blocking collectives  346 us (26%)
  local copies, waits for them, and re-layouts  64.8 us (5%)
  starting transfers between devices  57.6 us (4%)
  other arithmetic  32 us (2%)
  between operations  15.4 us (1%)
    psum x1, waiting for transfers between devices, on_device(): lax.psum((expand_part, project_part, bias_part, kernel_part), ('lon', 'la...  745 us
    psum x1, blocking collectives, on_device(): lax.psum((expand_part, project_part, bias_part, kernel_part), ('lon', 'la...  314 us
    unnamed x1, blocking collectives  32 us
    all_to_all x2, starting transfers between devices, extend(): tiles = lax.all_to_all(tiles, 'lon', split_axis=0, concat_axis=0)  27.5 us
  transfers between devices with their start and end apart: 14, of which 5 were waited for; matrix products, arithmetic and copies ran while one was open for 6% of the time, Pallas kernels for 0%

profile of v1, /device:TPU:4, one launch (start us, length us, event | category | flops | bytes accessed | tf_op | source)
XLA Modules:
  0.0 1317.7 jit_solution(15743403185017212462)
XLA Ops:
  10.3 15.2 %all-to-all-start = ((bf16[16,75,2,128]{3,2,1,0:T(2,128)(2,1)}), bf16[16,75,2,128]{3,2,1,0:T(2,128)(2,1)S(1)}, u32[]{:S(2)}, u32[]{:S(2)}) async-start(bf16[16,75,2,128]{3,2,1,0:T(2,128)(2,1)} %stack.36), calls=%async_computation | async-start | bytes 1228800 | tf_op jit(solution)/shard_map/all_to_all | solution.py:31
  25.8 3.4 scatter_custom_fusion
  33.2 3.8 collective-permute-start
  41.0 12.9 collective-permute-done
  56.6 3.5 collective-permute-start.2
  60.6 4.6 collective-permute-start.3
  67.2 5.5 rev.6
  73.3 4.0 concatenate.54
  82.6 4.1 fusion.19
  93.5 25.3 %all-gather.5.cloned.1.call-done = bf16[300,32,128]{2,1,0:T(8,128)(2,1)} async-done(((bf16[75,32,128]{2,1,0:T(8,128)(2,1)}), bf16[300,32,128]{2,1,0:T(8,128)(2,1)}) %all-gather.5.cloned.1.call-update) | async-done | bytes 2457616 | tf_op jit(solution)/shard_map/all_gather | solution.py:105
  129.7 32.0 %fusion = bf16[80,4096]{1,0:T(8,128)(2,1)} fusion(bf16[300,4096]{1,0:T(8,128)(2,1)} %fusion.2), kind=kCustom, calls=%all-reduce-scatter | all-reduce-scatter fusion | flops 1310721 | bytes 3115008
  165.4 5.0 collective-permute-done.8
  170.4 6.0 concatenate.62
  179.9 12.3 all-to-all-start.1
  192.3 3.2 convolution_multiply_fusion
  195.5 3.7 fusion.34
  204.7 5.1 collective-permute-start.5
  211.8 7.2 fusion.28
  223.1 3.4 collective-permute-start.7
  226.5 313.8 %all-reduce.2 = (f32[150]{0:T(256)}, f32[3,3,75]{2,1,0:T(4,128)}) all-reduce(f32[150]{0:T(256)S(1)} %copy-done.38, f32[3,3,75]{2,1,0:T(4,128)S(1)} %maximum_multiply_fusion), channel_id=1, replica_groups=mesh['lon'=16,'lat'=8,'ch'=4] {'lon','lat'}, use_global_device_ids=true, to_apply=%region_5.6 | all-reduce | flops 825 | bytes 6600 | tf_op jit(solution)/shard_map/psum | solution.py:172
  544.2 5.5 rev.7
  550.3 4.0 concatenate.57
  558.1 3.4 fusion.24
  563.0 744.8 %all-reduce.6.cloned.1.call-done = (f32[300,150]{0,1:T(8,128)}, f32[150,300]{1,0:T(8,128)}) async-done(((f32[300,150]{0,1:T(8,128)}, f32[150,300]{1,0:T(8,128)}), (f32[300,150]{0,1:T(8,128)}, f32[150,300]{1,0:T(8,128)})) %all-reduce.6.cloned.1.call-update) | async-done | bytes 360016 | tf_op jit(solution)/shard_map/psum | solution.py:172
  (166 shorter events, 70.5 us)
Async XLA Ops:
  7.2 115.0 %copy-start = (bf16[300,150]{0,1:T(8,128)(2,1)S(1)}, bf16[300,150]{0,1:T(8,128)(2,1)}, u32[]{:S(2)}) copy-start(bf16[300,150]{0,1:T(8,128)(2,1)} %param.19) | copy-start | bytes 270004
  9.1 16.5 %copy-start.17 = (bf16[75,32,128]{2,1,0:T(8,128)(2,1)S(1)}, bf16[75,32,128]{2,1,0:T(8,128)(2,1)}, u32[]{:S(2)}) copy-start(bf16[75,32,128]{2,1,0:T(8,128)(2,1)} %param.15) | copy-start | bytes 1843204
  10.3 56.3 %all-to-all-start = ((bf16[16,75,2,128]{3,2,1,0:T(2,128)(2,1)}), bf16[16,75,2,128]{3,2,1,0:T(2,128)(2,1)S(1)}, u32[]{:S(2)}, u32[]{:S(2)}) async-start(bf16[16,75,2,128]{3,2,1,0:T(2,128)(2,1)} %stack.36), calls=%async_computation | async-start | bytes 1228800 | tf_op jit(solution)/shard_map/all_to_all | solution.py:31
  25.5 63.2 %all-gather.3.cloned.1.call-start = ((), (), s32[]{:S(2)}) async-start(), calls=%async_computation.2 | async-start | bytes 3072000 | tf_op jit(solution)/shard_map/all_gather | solution.py:106
  30.3 88.5 %all-gather.5.cloned.1.call-start = ((), (), s32[]{:S(2)}) async-start(), calls=%async_computation.3 | async-start | bytes 3072000 | tf_op jit(solution)/shard_map/all_gather | solution.py:105
  33.2 20.7 %collective-permute-start = (bf16[75,32,2]{0,1,2:T(8,128)(2,1)S(1)}, bf16[75,32,2]{0,1,2:T(8,128)(2,1)S(1)}, u32[]{:S(2)}, u32[]{:S(2)}) collective-permute-start(bf16[75,32,2]{0,1,2:T(8,128)(2,1)S(1)} %copy.14), channel_id=1, source_target_pairs={{0,32},{32,64},{64,96},{96,128},{128,160},{160,192},{192,224},{224... | collective-permute-start | bytes 28808 | tf_op jit(solution)/shard_map/ppermute | solution.py:16
  37.8 17.2 %collective-permute-start.1 = (bf16[75,32,2]{0,1,2:T(8,128)(2,1)S(1)}, bf16[75,32,2]{0,1,2:T(8,128)(2,1)S(1)}, u32[]{:S(2)}, u32[]{:S(2)}) collective-permute-start(bf16[75,32,2]{0,1,2:T(8,128)(2,1)S(1)} %copy.15), channel_id=1, source_target_pairs={{32,0},{64,32},{96,64},{128,96},{160,128},{192,160},{224,192},{256... | collective-permute-start | bytes 28808 | tf_op jit(solution)/shard_map/ppermute | solution.py:19
  55.0 25.9 %copy-start.4 = (bf16[75,32,2]{2,1,0:T(8,128)(2,1)}, bf16[75,32,2]{2,1,0:T(8,128)(2,1)S(1)}, u32[]{:S(2)}) copy-start(bf16[75,32,2]{2,1,0:T(8,128)(2,1)S(1)} %copy.16) | copy-start | bytes 28804
  56.1 24.8 %copy-start.6 = (bf16[75,32,2]{2,1,0:T(8,128)(2,1)}, bf16[75,32,2]{2,1,0:T(8,128)(2,1)S(1)}, u32[]{:S(2)}) copy-start(bf16[75,32,2]{2,1,0:T(8,128)(2,1)S(1)} %copy.17) | copy-start | bytes 28804
  56.6 10.0 collective-permute-start.2
  60.6 20.3 %copy-start.19 = (f32[75]{0:T(128)}, f32[75]{0:T(128)S(1)}, u32[]{:S(2)}) copy-start(f32[75]{0:T(128)S(1)} %get-tuple-element.72) | copy-start | bytes 904
  60.6 20.3 %copy-start.21 = (f32[75]{0:T(128)}, f32[75]{0:T(128)S(1)}, u32[]{:S(2)}) copy-start(f32[75]{0:T(128)S(1)} %get-tuple-element.73) | copy-start | bytes 904
  60.6 20.3 %copy-start.23 = (f32[75]{0:T(128)}, f32[75]{0:T(128)S(1)}, u32[]{:S(2)}) copy-start(f32[75]{0:T(128)S(1)} %get-tuple-element.74) | copy-start | bytes 904
  60.6 20.3 %copy-start.25 = (f32[75]{0:T(128)}, f32[75]{0:T(128)S(1)}, u32[]{:S(2)}) copy-start(f32[75]{0:T(128)S(1)} %get-tuple-element.75) | copy-start | bytes 904
  60.6 20.3 %copy-start.27 = (f32[75]{0:T(128)}, f32[75]{0:T(128)S(1)}, u32[]{:S(2)}) copy-start(f32[75]{0:T(128)S(1)} %get-tuple-element.76) | copy-start | bytes 904
  60.6 20.3 %copy-start.29 = (f32[75]{0:T(128)}, f32[75]{0:T(128)S(1)}, u32[]{:S(2)}) copy-start(f32[75]{0:T(128)S(1)} %get-tuple-element.77) | copy-start | bytes 904
  60.6 16.7 %collective-permute-start.3 = (bf16[75,2,132]{2,1,0:T(2,128)(2,1)S(1)}, bf16[75,2,132]{2,1,0:T(2,128)(2,1)}, u32[]{:S(2)}, u32[]{:S(2)}) collective-permute-start(bf16[75,2,132]{2,1,0:T(2,128)(2,1)S(1)} %get-tuple-element.52), channel_id=1, source_target_pairs={{4,0},{8,4},{12,8},{16,12},{20,16},{24,20},{28,24},{0,28},{5,1},{9... | collective-permute-start | bytes 118808 | tf_op jit(solution)/shard_map/ppermute | solution.py:19
  162.7 7.8 collective-permute-start.8
  179.9 362.7 %all-to-all-start.1 = ((bf16[16,75,2,128]{3,2,1,0:T(2,128)(2,1)}), bf16[16,75,2,128]{3,2,1,0:T(2,128)(2,1)}, u32[]{:S(2)}, u32[]{:S(2)}) async-start(bf16[16,75,2,128]{3,2,1,0:T(2,128)(2,1)} %stack.37), calls=%async_computation.1 | async-start | bytes 1228800 | tf_op jit(solution)/shard_map/all_to_all | solution.py:31
  192.2 1115.7 %all-reduce.6.cloned.1.call-start = ((), (), s32[]{:S(2)}) async-start(), calls=%async_computation.4 | async-start | bytes 933888 | tf_op jit(solution)/shard_map/psum | solution.py:172
  204.7 16.2 %collective-permute-start.5 = (bf16[75,32,2]{0,1,2:T(8,128)(2,1)S(1)}, bf16[75,32,2]{0,1,2:T(8,128)(2,1)}, u32[]{:S(2)}, u32[]{:S(2)}) collective-permute-start(bf16[75,32,2]{0,1,2:T(8,128)(2,1)S(1)} %copy.22), channel_id=1, source_target_pairs={{32,0},{64,32},{96,64},{128,96},{160,128},{192,160},{224,192},{256... | collective-permute-start | bytes 28808 | tf_op jit(solution)/shard_map/ppermute | solution.py:19
  209.8 9.2 collective-permute-start.4
  223.1 319.4 %collective-permute-start.7 = (bf16[75,2,132]{2,1,0:T(2,128)(2,1)S(1)}, bf16[75,2,132]{2,1,0:T(2,128)(2,1)S(1)}, u32[]{:S(2)}, u32[]{:S(2)}) collective-permute-start(bf16[75,2,132]{2,1,0:T(2,128)(2,1)S(1)} %get-tuple-element.48), channel_id=1, source_target_pairs={{0,4},{4,8},{8,12},{12,16},{16,20},{20,24},{24,28},{28,0},{1,5},{5... | collective-permute-start | bytes 118808 | tf_op jit(solution)/shard_map/ppermute | solution.py:16
  540.3 14.0 %collective-permute-start.6 = (bf16[75,2,132]{2,1,0:T(2,128)(2,1)S(1)}, bf16[75,2,132]{2,1,0:T(2,128)(2,1)}, u32[]{:S(2)}, u32[]{:S(2)}) collective-permute-start(bf16[75,2,132]{2,1,0:T(2,128)(2,1)S(1)} %get-tuple-element.47), channel_id=1, source_target_pairs={{4,0},{8,4},{12,8},{16,12},{20,16},{24,20},{28,24},{0,28},{5,1},{9... | collective-permute-start | bytes 118808 | tf_op jit(solution)/shard_map/ppermute | solution.py:19
  (34 other events, 146.7 us)
Sparse Core Ops, SparseCore 0:
  30.5 35.2 all-gather.2
  86.9 31.9 all-gather.4
  199.4 1108.4 all-reduce.5
